TPU v7x, 256 devices: a whole 4x4x8 slice. The times are simulated.
256 devices in a mesh: aux: 16 (over z, core), occ: 4 (over y), vir: 4 (over x).
Axes of the slice: x: 4, y: 4, z: 8, core: 2. Of those that a mesh axis runs over, the one named last changes fastest.
Arguments:
- b_factors: bfloat16 [32, 3072, 8192], P('occ', 'vir', 'aux'), may hold values from -0.018310547 to 0.018310547
- right_side: float32 [32, 3072], P('occ', 'vir'), may hold values from -40 to 40
- occ_energy: float32 [32], P('occ'), may hold values from -3 to -0.5
- vir_energy: float32 [3072], P('vir'), may hold values from 0.5 to 6
Outputs:
- z_vector: float32 [32, 3072], P('occ', 'vir')
- residual: float32 [32, 3072], P('occ', 'vir')
All inputs are finite; a program needn't handle non-finite values.
Results may differ from a plain program's by a relative error of at most 0.023.
Values may be sent and summed in bfloat16 or wider, within the bound.
A program may use at most 64 MiB of HBM per device.

v0:
```python
import functools

import jax
import jax.numpy as jnp
from jax import lax
from jax.sharding import PartitionSpec as P

ITERS = 3


def copy_for_each(array, axis):
    copies = jnp.broadcast_to(array, (lax.axis_size(axis), *array.shape))
    return lax.all_to_all(copies, axis, split_axis=0, concat_axis=0, tiled=True)


def of_everyone(array, axis):
    everything = copy_for_each(array, axis)
    return jnp.sum(everything, axis=0)


def laid_out(parts, dim):
    parts = jnp.moveaxis(parts, 0, dim)
    lengths = parts.shape
    return parts.reshape(*lengths[:dim], lengths[dim] * lengths[dim + 1], *lengths[dim + 2 :])


def gather_directly(array, axis, dim):
    parts = copy_for_each(array, axis)
    return laid_out(parts, dim)


def cut_along(array, dim, peers):
    lengths = array.shape
    parts = array.reshape(*lengths[:dim], peers, lengths[dim] // peers, *lengths[dim + 1 :])
    return jnp.moveaxis(parts, dim, 0)


def sum_at_owner(array, axis, dim):
    parts = cut_along(array, dim, lax.axis_size(axis))
    arrived = lax.all_to_all(parts, axis, split_axis=0, concat_axis=0, tiled=True)
    return arrived.sum(axis=0)


def by_axis(array, axes):
    return functools.reduce(lax.psum, axes, array)


def respond(b_factors, trial, denom):
    trial_h = trial.astype(jnp.bfloat16)
    gamma_part = jnp.einsum("iaq,ia->q", b_factors, trial_h, preferred_element_type=jnp.float32)
    gamma = of_everyone(gamma_part, ("occ", "vir")).astype(jnp.bfloat16)
    coulomb = jnp.einsum("iaq,q->ia", b_factors, gamma, preferred_element_type=jnp.float32)
    pairs = jnp.einsum(
        "ibq,jb->ijq",
        b_factors,
        gather_directly(trial_h, "occ", 0),
        preferred_element_type=jnp.float32,
    )
    summed = of_everyone(pairs, "vir").astype(jnp.bfloat16)
    moved = lax.all_to_all(summed, "occ", split_axis=1, concat_axis=0, tiled=True)
    exchange_part = jnp.einsum("jaq,ijq->ia", b_factors, moved, preferred_element_type=jnp.float32)
    exchange_own = sum_at_owner(exchange_part, "occ", 0)
    coupling = of_everyone(4.0 * coulomb - exchange_own, "aux")
    return denom * trial + coupling


def paired_products(residual, precond, image):
    return (
        by_axis(jnp.sum(residual * precond), ("occ", "vir")),
        by_axis(jnp.sum(precond * image), ("occ", "vir")),
    )


def shards(b_factors, right_side, occ_energy, vir_energy):
    denom = vir_energy[None, :] - occ_energy[:, None]
    z_vector = jnp.zeros_like(right_side)
    residual = right_side
    precond = residual / denom
    image = respond(b_factors, precond, denom)
    rz_now, product = paired_products(residual, precond, image)
    alpha = rz_now / product
    direction, along = (precond, image)
    for step in range(ITERS):
        z_vector = z_vector + alpha * direction
        residual = residual - alpha * along
        if step + 1 < ITERS:
            precond = residual / denom
            image = respond(b_factors, precond, denom)
            rz_next, product = paired_products(residual, precond, image)
            ratio = rz_next / rz_now
            alpha = rz_next / (product - ratio * rz_next / alpha)
            direction = precond + ratio * direction
            along = image + ratio * along
            rz_now = rz_next
    return (z_vector, residual)


def solution(mesh):
    in_specs = (P("occ", "vir", "aux"), P("occ", "vir"), P("occ"), P("vir"))
    out_specs = (P("occ", "vir"), P("occ", "vir"))
    return jax.shard_map(shards, mesh=mesh, in_specs=in_specs, out_specs=out_specs, check_vma=False)
```

profile of v0, /device:TPU:1, one launch (start us, length us, event | category | flops | bytes accessed | tf_op | source)
XLA Modules:
  0.0 359.7 jit_solution(7876684461764081336)
XLA Ops:
  1.5 9.2 %all_to_all.123 = bf16[4,8,768]{2,1,0:T(8,128)(2,1)S(1)} all-to-all(bf16[4,8,768]{2,1,0:T(8,128)(2,1)S(1)} %broadcast_in_dim.39), channel_id=1, replica_groups=mesh['aux'=16,'occ'=4,'vir'=4] {'occ'}, dimensions={0} | all-to-all | bytes 98304 | tf_op jit(solution)/shard_map/all_to_all | solution.py:13
  10.7 4.0 %convolution_bitcast_fusion.2 = f32[8,32,512]{2,1,0:T(8,128)S(1)} fusion(bf16[8,768,512]{2,1,0:T(8,128)(2,1)} %param.4, bf16[4,8,768]{2,1,0:T(8,128)(2,1)S(1)} %all_to_all.123), kind=kOutput, calls=%fused_computation.8 | convolution fusion | flops 201326592 | bytes 6864896 | tf_op jit(solution)/shard_map/ibq,jb->ijq/dot_general | solution.py:53
  14.7 1.6 broadcast_in_dim.40
  16.3 4.0 %all-to-all-start.2 = ((f32[4,8,32,512]{3,2,1,0:T(8,128)}), f32[4,8,32,512]{3,2,1,0:T(8,128)S(1)}, u32[]{:S(2)}, u32[]{:S(2)}) async-start(f32[4,8,32,512]{3,2,1,0:T(8,128)} %broadcast_in_dim.40), calls=%async_computation.2 | async-start | bytes 4194304 | tf_op jit(solution)/shard_map/all_to_all | solution.py:13
  20.4 3.7 %fusion.28 = f32[1,512,1]{1,0,2:T(1,128)S(1)} fusion(bf16[8,768,512]{2,1,0:T(8,128)(2,1)} %param.4, bf16[8,768,1]{1,0,2:T(8,128)(2,1)S(1)} %fusion.51), kind=kOutput, calls=%fused_computation.34 | convolution fusion | flops 6291456 | bytes 6305792 | tf_op jit(solution)/shard_map/iaq,ia->q/dot_general | solution.py:50
  24.1 20.3 %all-to-all-done.2 = f32[4,8,32,512]{3,2,1,0:T(8,128)S(1)} async-done(((f32[4,8,32,512]{3,2,1,0:T(8,128)}), f32[4,8,32,512]{3,2,1,0:T(8,128)S(1)}, u32[]{:S(2)}, u32[]{:S(2)}) %all-to-all-start.2) | async-done | bytes 2097184 | tf_op jit(solution)/shard_map/all_to_all | solution.py:13
  45.0 3.5 all-to-all-start
  49.5 5.3 %all-to-all-done = f32[16,1,512]{2,1,0:T(1,128)S(1)} async-done(((f32[16,1,512]{2,1,0:T(1,128)}), f32[16,1,512]{2,1,0:T(1,128)S(1)}, u32[]{:S(2)}, u32[]{:S(2)}) %all-to-all-start) | async-done | bytes 32800 | tf_op jit(solution)/shard_map/all_to_all | solution.py:13
  54.9 3.4 all-to-all-start.3
  58.3 5.4 %all-to-all-done.3 = bf16[8,32,512]{2,0,1:T(8,128)(2,1)S(1)} async-done(((bf16[8,32,512]{2,0,1:T(8,128)(2,1)}), bf16[8,32,512]{2,0,1:T(8,128)(2,1)S(1)}, u32[]{:S(2)}, u32[]{:S(2)}) %all-to-all-start.3) | async-done | bytes 262176 | tf_op jit(solution)/shard_map/all_to_all | solution.py:60
  63.8 5.3 %fusion.6 = f32[4,8,768]{2,1,0:T(8,128)} fusion(bf16[4,8,8,512]{3,1,2,0:T(8,128)(2,1)S(1)} %bitcast.86, bf16[8,768,512]{2,1,0:T(8,128)(2,1)} %param.4), kind=kOutput, calls=%fused_computation.9 | convolution fusion | flops 201326592 | bytes 6651904 | tf_op jit(solution)/shard_map/jaq,ijq->ia/dot_general | solution.py:61
  69.1 3.3 all-to-all-start.4
  72.4 4.5 %fusion.33 = f32[1,8,768]{2,0,1:T(1,128)S(1)} fusion(bf16[512,1,1]{0,1,2:T(2,128)(2,1)S(1)} %reshape.41, bf16[8,768,512]{2,1,0:T(8,128)(2,1)} %param.4), kind=kOutput, calls=%fused_computation.50 | convolution fusion | flops 6291456 | bytes 6317056 | tf_op jit(solution)/shard_map/iaq,q->ia/dot_general | solution.py:52
  77.0 29.5 %all_to_all.124 = f32[16,8,768]{2,1,0:T(8,128)S(1)} all-to-all(f32[16,8,768]{2,1,0:T(8,128)S(1)} %broadcast_in_dim.41), channel_id=1, replica_groups=mesh['aux'=16,'occ'=4,'vir'=4] {'aux'}, dimensions={0} | all-to-all | bytes 786432 | tf_op jit(solution)/shard_map/all_to_all | solution.py:13
  107.2 8.3 %all-reduce.5 = (f32[]{:T(128)}, f32[]{:T(128)}) all-reduce(f32[]{:T(128)} %get-tuple-element.7, f32[]{:T(128)} %get-tuple-element.6), channel_id=1, replica_groups=mesh['aux'=16,'occ'=4,'vir'=4] {'occ'}, use_global_device_ids=true, to_apply=%region_1.0 | all-reduce | flops 2 | bytes 16 | tf_op jit(solution)/shard_map/psum | solution.py:45
  115.5 7.6 %all-reduce.2 = (f32[]{:T(128)}, f32[]{:T(128)}) all-reduce(f32[]{:T(128)} %get-tuple-element.18, f32[]{:T(128)} %get-tuple-element.19), channel_id=1, replica_groups=mesh['aux'=16,'occ'=4,'vir'=4] {'vir'}, use_global_device_ids=true, to_apply=%region_2.0 | all-reduce | flops 2 | bytes 16 | tf_op jit(solution)/shard_map/psum | solution.py:45
  124.6 6.7 %all_to_all.125 = bf16[4,8,768]{2,1,0:T(8,128)(2,1)S(1)} all-to-all(bf16[4,8,768]{2,1,0:T(8,128)(2,1)S(1)} %broadcast_in_dim.43), channel_id=1, replica_groups=mesh['aux'=16,'occ'=4,'vir'=4] {'occ'}, dimensions={0} | all-to-all | bytes 98304 | tf_op jit(solution)/shard_map/all_to_all | solution.py:13
  131.3 4.0 %convolution_bitcast_fusion.1 = f32[8,32,512]{2,1,0:T(8,128)S(1)} fusion(bf16[8,768,512]{2,1,0:T(8,128)(2,1)} %param.4, bf16[4,8,768]{2,1,0:T(8,128)(2,1)S(1)} %all_to_all.125), kind=kOutput, calls=%fused_computation.7 | convolution fusion | flops 201326592 | bytes 6864896 | tf_op jit(solution)/shard_map/ibq,jb->ijq/dot_general | solution.py:53
  135.3 1.6 broadcast_in_dim.44
  136.9 3.6 %all-to-all-start.8 = ((f32[4,8,32,512]{3,2,1,0:T(8,128)}), f32[4,8,32,512]{3,2,1,0:T(8,128)S(1)}, u32[]{:S(2)}, u32[]{:S(2)}) async-start(f32[4,8,32,512]{3,2,1,0:T(8,128)} %broadcast_in_dim.44), calls=%async_computation.8 | async-start | bytes 4194304 | tf_op jit(solution)/shard_map/all_to_all | solution.py:13
  140.5 3.7 %fusion.26 = f32[1,512,1]{1,0,2:T(1,128)S(1)} fusion(bf16[8,768,512]{2,1,0:T(8,128)(2,1)} %param.4, bf16[8,768,1]{1,0,2:T(8,128)(2,1)S(1)} %bitcast.90), kind=kOutput, calls=%fused_computation.32 | convolution fusion | flops 6291456 | bytes 6305792 | tf_op jit(solution)/shard_map/iaq,ia->q/dot_general | solution.py:50
  144.2 18.4 %all-to-all-done.8 = f32[4,8,32,512]{3,2,1,0:T(8,128)S(1)} async-done(((f32[4,8,32,512]{3,2,1,0:T(8,128)}), f32[4,8,32,512]{3,2,1,0:T(8,128)S(1)}, u32[]{:S(2)}, u32[]{:S(2)}) %all-to-all-start.8) | async-done | bytes 2097184 | tf_op jit(solution)/shard_map/all_to_all | solution.py:13
  163.2 3.5 all-to-all-start.6
  167.8 5.3 %all-to-all-done.6 = f32[16,1,512]{2,1,0:T(1,128)S(1)} async-done(((f32[16,1,512]{2,1,0:T(1,128)}), f32[16,1,512]{2,1,0:T(1,128)S(1)}, u32[]{:S(2)}, u32[]{:S(2)}) %all-to-all-start.6) | async-done | bytes 32800 | tf_op jit(solution)/shard_map/all_to_all | solution.py:13
  173.1 3.4 all-to-all-start.9
  176.5 5.4 %all-to-all-done.9 = bf16[8,32,512]{2,0,1:T(8,128)(2,1)S(1)} async-done(((bf16[8,32,512]{2,0,1:T(8,128)(2,1)}), bf16[8,32,512]{2,0,1:T(8,128)(2,1)S(1)}, u32[]{:S(2)}, u32[]{:S(2)}) %all-to-all-start.9) | async-done | bytes 262176 | tf_op jit(solution)/shard_map/all_to_all | solution.py:60
  182.0 5.3 %fusion.9 = f32[4,8,768]{2,1,0:T(8,128)} fusion(bf16[4,8,8,512]{3,1,2,0:T(8,128)(2,1)S(1)} %bitcast.87, bf16[8,768,512]{2,1,0:T(8,128)(2,1)} %param.4), kind=kOutput, calls=%fused_computation.10 | convolution fusion | flops 201326592 | bytes 6651904 | tf_op jit(solution)/shard_map/jaq,ijq->ia/dot_general | solution.py:61
  187.3 3.3 all-to-all-start.10
  190.6 4.5 %fusion.34 = f32[1,8,768]{2,0,1:T(1,128)S(1)} fusion(bf16[512,1,1]{0,1,2:T(2,128)(2,1)S(1)} %reshape.48, bf16[8,768,512]{2,1,0:T(8,128)(2,1)} %param.4), kind=kOutput, calls=%fused_computation.51 | convolution fusion | flops 6291456 | bytes 6317056 | tf_op jit(solution)/shard_map/iaq,q->ia/dot_general | solution.py:52
  195.3 25.6 %all_to_all.126 = f32[16,8,768]{2,1,0:T(8,128)S(1)} all-to-all(f32[16,8,768]{2,1,0:T(8,128)S(1)} %broadcast_in_dim.45), channel_id=1, replica_groups=mesh['aux'=16,'occ'=4,'vir'=4] {'aux'}, dimensions={0} | all-to-all | bytes 786432 | tf_op jit(solution)/shard_map/all_to_all | solution.py:13
  221.6 8.4 %all-reduce.4 = (f32[]{:T(128)}, f32[]{:T(128)}) all-reduce(f32[]{:T(128)} %get-tuple-element.5, f32[]{:T(128)} %get-tuple-element.4), channel_id=1, replica_groups=mesh['aux'=16,'occ'=4,'vir'=4] {'occ'}, use_global_device_ids=true, to_apply=%region_11.0 | all-reduce | flops 2 | bytes 16 | tf_op jit(solution)/shard_map/psum | solution.py:45
  230.0 7.6 %all-reduce.1 = (f32[]{:T(128)}, f32[]{:T(128)}) all-reduce(f32[]{:T(128)} %get-tuple-element.16, f32[]{:T(128)} %get-tuple-element.17), channel_id=1, replica_groups=mesh['aux'=16,'occ'=4,'vir'=4] {'vir'}, use_global_device_ids=true, to_apply=%region_12.0 | all-reduce | flops 2 | bytes 16 | tf_op jit(solution)/shard_map/psum | solution.py:45
  242.2 6.7 %all_to_all.127 = bf16[4,8,768]{2,1,0:T(8,128)(2,1)S(1)} all-to-all(bf16[4,8,768]{2,1,0:T(8,128)(2,1)S(1)} %broadcast_in_dim.47), channel_id=1, replica_groups=mesh['aux'=16,'occ'=4,'vir'=4] {'occ'}, dimensions={0} | all-to-all | bytes 98304 | tf_op jit(solution)/shard_map/all_to_all | solution.py:13
  249.0 4.0 %convolution_bitcast_fusion = f32[8,32,512]{2,1,0:T(8,128)S(1)} fusion(bf16[8,768,512]{2,1,0:T(8,128)(2,1)} %param.4, bf16[4,8,768]{2,1,0:T(8,128)(2,1)S(1)} %all_to_all.127), kind=kOutput, calls=%fused_computation.6 | convolution fusion | flops 201326592 | bytes 6864896 | tf_op jit(solution)/shard_map/ibq,jb->ijq/dot_general | solution.py:53
  252.9 1.6 broadcast_in_dim.48
  254.5 3.6 %all-to-all-start.14 = ((f32[4,8,32,512]{3,2,1,0:T(8,128)}), f32[4,8,32,512]{3,2,1,0:T(8,128)S(1)}, u32[]{:S(2)}, u32[]{:S(2)}) async-start(f32[4,8,32,512]{3,2,1,0:T(8,128)} %broadcast_in_dim.48), calls=%async_computation.14 | async-start | bytes 4194304 | tf_op jit(solution)/shard_map/all_to_all | solution.py:13
  258.2 3.7 %fusion.24 = f32[1,512,1]{1,0,2:T(1,128)S(1)} fusion(bf16[8,768,512]{2,1,0:T(8,128)(2,1)} %param.4, bf16[8,768,1]{1,0,2:T(8,128)(2,1)S(1)} %bitcast.89), kind=kOutput, calls=%fused_computation.30 | convolution fusion | flops 6291456 | bytes 6305792 | tf_op jit(solution)/shard_map/iaq,ia->q/dot_general | solution.py:50
  261.9 18.4 %all-to-all-done.14 = f32[4,8,32,512]{3,2,1,0:T(8,128)S(1)} async-done(((f32[4,8,32,512]{3,2,1,0:T(8,128)}), f32[4,8,32,512]{3,2,1,0:T(8,128)S(1)}, u32[]{:S(2)}, u32[]{:S(2)}) %all-to-all-start.14) | async-done | bytes 2097184 | tf_op jit(solution)/shard_map/all_to_all | solution.py:13
  280.9 3.5 all-to-all-start.12
  285.4 5.3 %all-to-all-done.12 = f32[16,1,512]{2,1,0:T(1,128)S(1)} async-done(((f32[16,1,512]{2,1,0:T(1,128)}), f32[16,1,512]{2,1,0:T(1,128)S(1)}, u32[]{:S(2)}, u32[]{:S(2)}) %all-to-all-start.12) | async-done | bytes 32800 | tf_op jit(solution)/shard_map/all_to_all | solution.py:13
  290.7 3.4 all-to-all-start.15
  294.2 5.4 %all-to-all-done.15 = bf16[8,32,512]{2,0,1:T(8,128)(2,1)S(1)} async-done(((bf16[8,32,512]{2,0,1:T(8,128)(2,1)}), bf16[8,32,512]{2,0,1:T(8,128)(2,1)S(1)}, u32[]{:S(2)}, u32[]{:S(2)}) %all-to-all-start.15) | async-done | bytes 262176 | tf_op jit(solution)/shard_map/all_to_all | solution.py:60
  299.6 5.3 %fusion.12 = f32[4,8,768]{2,1,0:T(8,128)} fusion(bf16[4,8,8,512]{3,1,2,0:T(8,128)(2,1)S(1)} %bitcast.88, bf16[8,768,512]{2,1,0:T(8,128)(2,1)} %param.4), kind=kOutput, calls=%fused_computation.11 | convolution fusion | flops 201326592 | bytes 6651904 | tf_op jit(solution)/shard_map/jaq,ijq->ia/dot_general | solution.py:61
  304.9 3.3 all-to-all-start.16
  308.2 4.5 %fusion.35 = f32[1,8,768]{2,0,1:T(1,128)S(1)} fusion(bf16[512,1,1]{0,1,2:T(2,128)(2,1)S(1)} %reshape.54, bf16[8,768,512]{2,1,0:T(8,128)(2,1)} %param.4), kind=kOutput, calls=%fused_computation.52 | convolution fusion | flops 6291456 | bytes 6317056 | tf_op jit(solution)/shard_map/iaq,q->ia/dot_general | solution.py:52
  312.9 25.6 %all_to_all.128 = f32[16,8,768]{2,1,0:T(8,128)S(1)} all-to-all(f32[16,8,768]{2,1,0:T(8,128)S(1)} %broadcast_in_dim.49), channel_id=1, replica_groups=mesh['aux'=16,'occ'=4,'vir'=4] {'aux'}, dimensions={0} | all-to-all | bytes 786432 | tf_op jit(solution)/shard_map/all_to_all | solution.py:13
  339.2 8.3 %all-reduce.3 = (f32[]{:T(128)}, f32[]{:T(128)}) all-reduce(f32[]{:T(128)} %get-tuple-element.3, f32[]{:T(128)} %get-tuple-element.2), channel_id=1, replica_groups=mesh['aux'=16,'occ'=4,'vir'=4] {'occ'}, use_global_device_ids=true, to_apply=%region_21.0 | all-reduce | flops 2 | bytes 16 | tf_op jit(solution)/shard_map/psum | solution.py:45
  347.5 7.6 %all-reduce = (f32[]{:T(128)}, f32[]{:T(128)}) all-reduce(f32[]{:T(128)} %get-tuple-element.14, f32[]{:T(128)} %get-tuple-element.15), channel_id=1, replica_groups=mesh['aux'=16,'occ'=4,'vir'=4] {'vir'}, use_global_device_ids=true, to_apply=%region_22.0 | all-reduce | flops 2 | bytes 16 | tf_op jit(solution)/shard_map/psum | solution.py:45
  (47 shorter events, 9.7 us)
Async XLA Ops:
  10.7 9.7 %copy-start = (f32[8,768]{1,0:T(8,128)S(1)}, f32[8,768]{1,0:T(8,128)}, u32[]{:S(2)}) copy-start(f32[8,768]{1,0:T(8,128)} %param.5) | copy-start | bytes 73732
  10.7 9.7 %copy-start.1 = (f32[768]{0:T(1024)S(1)}, f32[768]{0:T(1024)}, u32[]{:S(2)}) copy-start(f32[768]{0:T(1024)} %param.7) | copy-start | bytes 9220
  10.7 9.7 %copy-start.2 = (f32[8]{0:T(128)S(1)}, f32[8]{0:T(128)}, u32[]{:S(2)}) copy-start(f32[8]{0:T(128)} %param.6) | copy-start | bytes 100
  16.3 28.1 %all-to-all-start.2 = ((f32[4,8,32,512]{3,2,1,0:T(8,128)}), f32[4,8,32,512]{3,2,1,0:T(8,128)S(1)}, u32[]{:S(2)}, u32[]{:S(2)}) async-start(f32[4,8,32,512]{3,2,1,0:T(8,128)} %broadcast_in_dim.40), calls=%async_computation.2 | async-start | bytes 4194304 | tf_op jit(solution)/shard_map/all_to_all | solution.py:13
  45.0 9.9 %all-to-all-start = ((f32[16,1,512]{2,1,0:T(1,128)}), f32[16,1,512]{2,1,0:T(1,128)S(1)}, u32[]{:S(2)}, u32[]{:S(2)}) async-start(f32[16,1,512]{2,1,0:T(1,128)} %broadcast_in_dim.38), calls=%async_computation | async-start | bytes 65536 | tf_op jit(solution)/shard_map/all_to_all | solution.py:13
  54.9 8.9 %all-to-all-start.3 = ((bf16[8,32,512]{2,0,1:T(8,128)(2,1)}), bf16[8,32,512]{2,0,1:T(8,128)(2,1)S(1)}, u32[]{:S(2)}, u32[]{:S(2)}) async-start(bf16[8,32,512]{2,0,1:T(8,128)(2,1)} %copy.10), calls=%async_computation.3 | async-start | bytes 524288 | tf_op jit(solution)/shard_map/all_to_all | solution.py:60
  69.1 7.9 %all-to-all-start.4 = ((f32[4,8,768]{2,1,0:T(8,128)}), f32[4,8,768]{2,1,0:T(8,128)S(1)}, u32[]{:S(2)}, u32[]{:S(2)}) async-start(f32[4,8,768]{2,1,0:T(8,128)} %fusion.6), calls=%async_computation.4 | async-start | bytes 196608 | tf_op jit(solution)/shard_map/all_to_all | solution.py:40
  136.9 25.7 %all-to-all-start.8 = ((f32[4,8,32,512]{3,2,1,0:T(8,128)}), f32[4,8,32,512]{3,2,1,0:T(8,128)S(1)}, u32[]{:S(2)}, u32[]{:S(2)}) async-start(f32[4,8,32,512]{3,2,1,0:T(8,128)} %broadcast_in_dim.44), calls=%async_computation.8 | async-start | bytes 4194304 | tf_op jit(solution)/shard_map/all_to_all | solution.py:13
  163.2 9.9 %all-to-all-start.6 = ((f32[16,1,512]{2,1,0:T(1,128)}), f32[16,1,512]{2,1,0:T(1,128)S(1)}, u32[]{:S(2)}, u32[]{:S(2)}) async-start(f32[16,1,512]{2,1,0:T(1,128)} %broadcast_in_dim.42), calls=%async_computation.6 | async-start | bytes 65536 | tf_op jit(solution)/shard_map/all_to_all | solution.py:13
  173.1 8.9 %all-to-all-start.9 = ((bf16[8,32,512]{2,0,1:T(8,128)(2,1)}), bf16[8,32,512]{2,0,1:T(8,128)(2,1)S(1)}, u32[]{:S(2)}, u32[]{:S(2)}) async-start(bf16[8,32,512]{2,0,1:T(8,128)(2,1)} %copy.12), calls=%async_computation.9 | async-start | bytes 524288 | tf_op jit(solution)/shard_map/all_to_all | solution.py:60
  187.3 7.9 %all-to-all-start.10 = ((f32[4,8,768]{2,1,0:T(8,128)}), f32[4,8,768]{2,1,0:T(8,128)S(1)}, u32[]{:S(2)}, u32[]{:S(2)}) async-start(f32[4,8,768]{2,1,0:T(8,128)} %fusion.9), calls=%async_computation.10 | async-start | bytes 196608 | tf_op jit(solution)/shard_map/all_to_all | solution.py:40
  254.5 25.7 %all-to-all-start.14 = ((f32[4,8,32,512]{3,2,1,0:T(8,128)}), f32[4,8,32,512]{3,2,1,0:T(8,128)S(1)}, u32[]{:S(2)}, u32[]{:S(2)}) async-start(f32[4,8,32,512]{3,2,1,0:T(8,128)} %broadcast_in_dim.48), calls=%async_computation.14 | async-start | bytes 4194304 | tf_op jit(solution)/shard_map/all_to_all | solution.py:13
  280.9 9.9 %all-to-all-start.12 = ((f32[16,1,512]{2,1,0:T(1,128)}), f32[16,1,512]{2,1,0:T(1,128)S(1)}, u32[]{:S(2)}, u32[]{:S(2)}) async-start(f32[16,1,512]{2,1,0:T(1,128)} %broadcast_in_dim.46), calls=%async_computation.12 | async-start | bytes 65536 | tf_op jit(solution)/shard_map/all_to_all | solution.py:13
  290.7 8.9 %all-to-all-start.15 = ((bf16[8,32,512]{2,0,1:T(8,128)(2,1)}), bf16[8,32,512]{2,0,1:T(8,128)(2,1)S(1)}, u32[]{:S(2)}, u32[]{:S(2)}) async-start(bf16[8,32,512]{2,0,1:T(8,128)(2,1)} %copy.14), calls=%async_computation.15 | async-start | bytes 524288 | tf_op jit(solution)/shard_map/all_to_all | solution.py:60
  304.9 7.9 %all-to-all-start.16 = ((f32[4,8,768]{2,1,0:T(8,128)}), f32[4,8,768]{2,1,0:T(8,128)S(1)}, u32[]{:S(2)}, u32[]{:S(2)}) async-start(f32[4,8,768]{2,1,0:T(8,128)} %fusion.12), calls=%async_computation.16 | async-start | bytes 196608 | tf_op jit(solution)/shard_map/all_to_all | solution.py:40
where the time goes:
time: 363 us; the launch traced here: 360 us
  blocking collectives  151 us (42%)
  waiting for transfers between devices  89.6 us (25%)
  matrix products  52.4 us (14%)
  starting transfers between devices  41.8 us (12%)
  between operations  10.6 us (3%)
  local copies, waits for them, and re-layouts  9.39 us (3%)
  other arithmetic  4.9 us (1%)
    all_to_all x6, blocking collectives, copy_for_each(): return lax.all_to_all(copies, axis, split_axis=0, concat_axis=0, tiled=True)  103 us
    all_to_all x6, waiting for transfers between devices, copy_for_each(): return lax.all_to_all(copies, axis, split_axis=0, concat_axis=0, tiled=True)  72.9 us
    psum x6, blocking collectives, by_axis(): return functools.reduce(lax.psum, axes, array)  47.7 us
    all_to_all x6, starting transfers between devices, copy_for_each(): return lax.all_to_all(copies, axis, split_axis=0, concat_axis=0, tiled=True)  21.7 us
    all_to_all x3, waiting for transfers between devices, respond(): lax.all_to_all(summed, 'occ', split_axis=1, concat_axis=0, tiled=True)  16.3 us
    dot_general x3, matrix products, respond(): jnp.einsum('jaq,ijq->ia', b_factors, moved, preferred_element_type=jnp.fl...  15.9 us
    dot_general x3, matrix products, respond(): jnp.einsum('iaq,q->ia', b_factors, gamma, preferred_element_type=jnp.floa...  13.5 us
    dot_general x3, matrix products, respond(): jnp.einsum('ibq,jb->ijq', b_factors, gather_directly(trial_h, 'occ', 0),...  11.9 us
  transfers between devices with their start and end apart: 12, of which 12 were waited for; matrix products, arithmetic and copies ran while one was open for 8% of the time, Pallas kernels for 0%

commit v1 on v0

v1 whole, which is shorter than its diff:
```python
import functools

import jax
import jax.numpy as jnp
from jax import lax
from jax.experimental import pallas as pl
from jax.experimental.pallas import tpu as pltpu
from jax.sharding import PartitionSpec as P

ITERS = 3
MESH = pl.DeviceIdType.MESH
LANES = 128
ROWS = 8


def wait_bytes(ref, sem):
    pltpu.make_async_copy(ref, ref, sem).wait()


def kernel(
    sizes,
    b_hbm,
    right_ref,
    denom_ref,
    z_out,
    residual_out,
    b_ref,
    r_full,
    d_full,
    xh_ref,
    z_ref,
    x_ref,
    dir_ref,
    along_ref,
    p1_send,
    p1_recv,
    sums_ref,
    pairs_ref,
    gamma_ref,
    acc_ref,
    e_ref,
    rs_recv,
    total_ref,
    dots_ref,
    b_sem,
    init_sem,
    sems,
):
    n_aux, n_occ, n_vir = sizes
    aux, occ, vir = lax.axis_index("aux"), lax.axis_index("occ"), lax.axis_index("vir")
    n_i, n_a, n_p = b_ref.shape
    tiles = n_a // LANES
    n_all = n_occ * n_i
    plane, column = n_occ * n_vir, n_aux * n_occ
    quarter = n_p // n_vir
    owners = [(k * n_aux) // tiles for k in range(tiles)]

    def device(aux_at, occ_at, vir_at):
        return {"aux": aux_at, "occ": occ_at, "vir": vir_at}

    def send(src, dst, send_sem, recv_sem, where):
        pltpu.make_async_remote_copy(
            src_ref=src,
            dst_ref=dst,
            send_sem=send_sem,
            recv_sem=recv_sem,
            device_id=where,
            device_id_type=MESH,
        ).start()

    def plane_peer(step):
        return lax.rem(occ + step // n_vir, n_occ), lax.rem(vir + step % n_vir, n_vir)

    def column_peer(step):
        place = lax.rem(aux * n_occ + occ + step, column)
        return place // n_occ, lax.rem(place, n_occ)

    def load(i):
        return pltpu.make_async_copy(b_hbm.at[i], b_ref.at[i], b_sem.at[i])

    for i in range(n_i):
        load(i).start()

    barrier = pltpu.get_barrier_semaphore()

    @pl.loop(1, column)
    def _(step):
        aux_at, occ_at = column_peer(step)
        pl.semaphore_signal(barrier, inc=1, device_id=device(aux_at, occ_at, vir), device_id_type=MESH)

    for step in range(1, plane):
        if step % n_vir:
            occ_at, vir_at = plane_peer(step)
            pl.semaphore_signal(barrier, inc=1, device_id=device(aux, occ_at, vir_at), device_id_type=MESH)

    for k in range(tiles):
        cut = slice(k * LANES, (k + 1) * LANES)
        r_full[occ, k] = right_ref[:, cut]
        d_full[occ, k] = denom_ref[:, cut]

    pl.semaphore_wait(barrier, column - 1 + n_occ * (n_vir - 1))

    for step in range(1, n_occ):
        where = device(aux, lax.rem(occ + step, n_occ), vir)
        send(r_full.at[occ], r_full.at[occ], init_sem.at[0], init_sem.at[1], where)
        send(d_full.at[occ], d_full.at[occ], init_sem.at[2], init_sem.at[3], where)
    others = pl.ds(0, n_occ - 1)
    wait_bytes(r_full.at[others], init_sem.at[1])
    wait_bytes(d_full.at[others], init_sem.at[3])
    wait_bytes(r_full.at[others], init_sem.at[0])
    wait_bytes(d_full.at[others], init_sem.at[2])

    is_owner = functools.reduce(jnp.logical_or, [aux == owner for owner in owners])
    my_tile = occ * tiles + sum(jnp.where(aux == owner, k, 0) for k, owner in enumerate(owners))
    flat = (n_occ * tiles, ROWS, LANES)

    z_ref[...] = jnp.zeros_like(z_ref)
    rz_now = alpha = None

    for turn in range(ITERS):
        sem = functools.partial(lambda turn, index: sems.at[turn, index], turn)

        x = r_full[...] / d_full[...]
        x_ref[...] = x
        for o in range(0, n_occ, 2):
            for k in range(tiles):
                both = jnp.concatenate([x[o, k], x[o + 1, k]], axis=0)
                xh_ref[o * ROWS : (o + 2) * ROWS, k * LANES : (k + 1) * LANES] = both.astype(jnp.bfloat16)

        mine = p1_recv.at[turn, occ * n_vir + vir]
        xh = xh_ref[...]

        @pl.loop(0, n_i // 2)
        def _(half):
            i = half * 2
            if turn == 0:
                load(i).wait()
                load(i + 1).wait()
            one = jnp.dot(xh, b_ref[i], preferred_element_type=jnp.float32)
            two = jnp.dot(xh, b_ref[i + 1], preferred_element_type=jnp.float32)
            rows = pl.ds(pl.multiple_of(half * 2 * ROWS, 2 * ROWS), 2 * ROWS)
            for o in range(n_occ):
                for q in range(n_vir):
                    cut = (slice(o * ROWS, (o + 1) * ROWS), slice(q * quarter, (q + 1) * quarter))
                    both = jnp.concatenate([one[cut], two[cut]], axis=0).astype(jnp.bfloat16)
                    p1_send[turn, o * n_vir + q, rows, :] = both

        for step in range(1, plane):
            occ_at, vir_at = plane_peer(step)
            send(
                p1_send.at[turn, occ_at * n_vir + vir_at],
                p1_recv.at[turn, occ * n_vir + vir],
                sem(0),
                sem(1),
                device(aux, occ_at, vir_at),
            )
        mine[...] = p1_send[turn, occ * n_vir + vir]
        wait_bytes(p1_recv.at[turn, pl.ds(0, plane - 1)], sem(1))

        for o in range(n_occ):
            total = p1_recv[turn, o * n_vir].astype(jnp.float32)
            for v in range(1, n_vir):
                total = total + p1_recv[turn, o * n_vir + v].astype(jnp.float32)
            sums_ref[o * n_i * ROWS : (o + 1) * n_i * ROWS, :] = total
        for j in range(ROWS):
            column_j = sums_ref[pl.ds(j, n_all, stride=ROWS), :]
            pairs_ref[turn, vir, j * n_all : (j + 1) * n_all, :] = column_j.astype(jnp.bfloat16)
        for step in range(1, n_vir):
            send(
                pairs_ref.at[turn, vir],
                pairs_ref.at[turn, vir],
                sem(2),
                sem(3),
                device(aux, occ, lax.rem(vir + step, n_vir)),
            )
        diagonal = sums_ref[pl.ds(occ * n_i * ROWS, ROWS, stride=ROWS + 1), :]
        gamma_ref[turn, occ * n_vir + vir] = jnp.sum(diagonal, axis=0, keepdims=True)
        for step in range(1, plane):
            occ_at, vir_at = plane_peer(step)
            at = gamma_ref.at[turn, occ * n_vir + vir]
            send(at, at, sem(4), sem(5), device(aux, occ_at, vir_at))

        wait_bytes(pairs_ref.at[turn, pl.ds(0, n_vir - 1)], sem(3))
        wait_bytes(gamma_ref.at[turn, pl.ds(0, plane - 1)], sem(5))
        gamma = []
        for q in range(n_vir):
            parts = [gamma_ref[turn, o * n_vir + q] for o in range(n_occ)]
            gamma.append(functools.reduce(jnp.add, parts))
        gamma = jnp.concatenate(gamma, axis=1)
        gamma = jnp.broadcast_to(gamma, (2 * ROWS, n_p))
        row = lax.broadcasted_iota(jnp.int32, (2 * ROWS, n_p), 0)
        acc_ref[...] = jnp.zeros_like(acc_ref)

        @pl.loop(0, ROWS)
        def _(j):
            rows = pl.ds(pl.multiple_of(j * n_all, n_all), n_all)
            left = jnp.concatenate([pairs_ref[turn, q, rows, :] for q in range(n_vir)], axis=1)
            below = jnp.where(row == j, gamma, 0.0).astype(jnp.bfloat16)
            left = jnp.concatenate([left, below], axis=0)
            acc_ref[...] += lax.dot_general(
                left, b_ref[j], (((1,), (1,)), ((), ())), preferred_element_type=jnp.float32
            )

        for o in range(n_occ):
            for k in range(tiles):
                cut = (slice(o * ROWS, (o + 1) * ROWS), slice(k * LANES, (k + 1) * LANES))
                e_ref[turn, o * tiles + k] = -acc_ref[cut]
        for k in range(tiles):
            coulomb = acc_ref[n_all : n_all + ROWS, k * LANES : (k + 1) * LANES]
            e_ref[turn, occ * tiles + k] += 4.0 * coulomb

        place = aux * n_occ + occ
        for o in range(n_occ):
            for k in range(tiles):
                here = jnp.logical_and(occ == o, aux == owners[k])

                @pl.when(jnp.logical_not(here))
                def _():
                    send(
                        e_ref.at[turn, o * tiles + k],
                        rs_recv.at[turn, place],
                        sem(6),
                        sem(7),
                        device(owners[k], o, vir),
                    )

        n_tiles = n_occ * tiles

        @pl.when(is_owner)
        def _():
            rs_recv[turn, place] = e_ref[turn, my_tile]
            wait_bytes(rs_recv.at[turn, pl.ds(0, column - 1)], sem(7))
            parts = [jnp.zeros((ROWS, LANES), jnp.float32) for _ in range(4)]
            for source in range(column):
                parts[source % 4] = parts[source % 4] + rs_recv[turn, source]
            total_ref[turn, my_tile] = (parts[0] + parts[1]) + (parts[2] + parts[3])

            @pl.loop(1, column)
            def _(step):
                aux_at, occ_at = column_peer(step)
                at = total_ref.at[turn, my_tile]
                send(at, at, sem(8), sem(9), device(aux_at, occ_at, vir))

            wait_bytes(total_ref.at[turn, pl.ds(0, n_tiles - 1)], sem(9))

        @pl.when(jnp.logical_not(is_owner))
        def _():
            wait_bytes(total_ref.at[turn], sem(9))

        x = x_ref[...].reshape(flat)
        image = d_full[...].reshape(flat) * x + total_ref[turn]
        dots_ref[turn, vir, 0] = jnp.sum(r_full[...].reshape(flat) * x, axis=0)
        dots_ref[turn, vir, 1] = jnp.sum(x * image, axis=0)
        for step in range(1, n_vir):
            at = dots_ref.at[turn, vir]
            send(at, at, sem(10), sem(11), device(aux, occ, lax.rem(vir + step, n_vir)))
        wait_bytes(dots_ref.at[turn, pl.ds(0, n_vir - 1)], sem(11))
        dots = functools.reduce(jnp.add, [dots_ref[turn, v] for v in range(n_vir)])
        rz_next = jnp.sum(dots[0], keepdims=True)
        product = jnp.sum(dots[1], keepdims=True)

        if turn == 0:
            alpha = rz_next / product
            direction, along = x, image
        else:
            ratio = rz_next / rz_now
            alpha = rz_next / (product - ratio * rz_next / alpha)
            direction = x + ratio[None] * dir_ref[...].reshape(flat)
            along = image + ratio[None] * along_ref[...].reshape(flat)
        rz_now = rz_next
        shape = r_full.shape
        if turn + 1 < ITERS:
            dir_ref[...] = direction.reshape(shape)
            along_ref[...] = along.reshape(shape)
        z_ref[...] += (alpha[None] * direction).reshape(shape)
        r_full[...] -= (alpha[None] * along).reshape(shape)

    for k in range(tiles):
        cut = slice(k * LANES, (k + 1) * LANES)
        z_out[:, cut] = z_ref[occ, k]
        residual_out[:, cut] = r_full[occ, k]

    n_tiles = n_occ * tiles
    for turn in range(ITERS):
        wait_bytes(p1_send.at[turn, pl.ds(0, plane - 1)], sems.at[turn, 0])
        wait_bytes(pairs_ref.at[turn, pl.ds(0, n_vir - 1)], sems.at[turn, 2])
        wait_bytes(gamma_ref.at[turn, pl.ds(0, plane - 1)], sems.at[turn, 4])
        wait_bytes(dots_ref.at[turn, pl.ds(0, n_vir - 1)], sems.at[turn, 10])

    @pl.when(is_owner)
    def _():
        for turn in range(ITERS):
            wait_bytes(e_ref.at[turn, pl.ds(0, n_tiles - 1)], sems.at[turn, 6])
            wait_bytes(rs_recv.at[turn, pl.ds(0, column - 1)], sems.at[turn, 8])

    @pl.when(jnp.logical_not(is_owner))
    def _():
        for turn in range(ITERS):
            wait_bytes(e_ref.at[turn], sems.at[turn, 6])


def solution(mesh):
    sizes = tuple(mesh.shape[name] for name in ("aux", "occ", "vir"))
    n_aux, n_occ, n_vir = sizes

    def shards(b_factors, right_side, occ_energy, vir_energy):
        n_i, n_a, n_p = b_factors.shape
        tiles = n_a // LANES
        plane, column = n_occ * n_vir, n_aux * n_occ
        n_all = n_occ * n_i
        denom = vir_energy[None, :] - occ_energy[:, None]
        f32, bf16 = jnp.float32, jnp.bfloat16
        whole = pltpu.VMEM((n_occ, tiles, ROWS, LANES), f32)
        vmem = pl.BlockSpec(memory_space=pltpu.VMEM)
        return tuple(
            pl.pallas_call(
                functools.partial(kernel, sizes),
                out_shape=[jax.ShapeDtypeStruct((n_i, n_a), f32)] * 2,
                in_specs=[pl.BlockSpec(memory_space=pl.ANY), vmem, vmem],
                out_specs=[vmem, vmem],
                scratch_shapes=[
                    pltpu.VMEM((n_i, n_a, n_p), bf16),
                    whole,
                    whole,
                    pltpu.VMEM((n_all, n_a), bf16),
                    whole,
                    whole,
                    whole,
                    whole,
                    pltpu.VMEM((ITERS, plane, n_i * ROWS, LANES), bf16),
                    pltpu.VMEM((ITERS, plane, n_i * ROWS, LANES), bf16),
                    pltpu.VMEM((n_all * ROWS, LANES), f32),
                    pltpu.VMEM((ITERS, n_vir, n_all * ROWS, LANES), bf16),
                    pltpu.VMEM((ITERS, plane, 1, LANES), f32),
                    pltpu.VMEM((n_all + 2 * ROWS, n_a), f32),
                    pltpu.VMEM((ITERS, n_occ * tiles, ROWS, LANES), f32),
                    pltpu.VMEM((ITERS, column, ROWS, LANES), f32),
                    pltpu.VMEM((ITERS, n_occ * tiles, ROWS, LANES), f32),
                    pltpu.VMEM((ITERS, n_vir, 2, ROWS, LANES), f32),
                    pltpu.SemaphoreType.DMA((n_i,)),
                    pltpu.SemaphoreType.DMA((4,)),
                    pltpu.SemaphoreType.DMA((ITERS, 12)),
                ],
                compiler_params=pltpu.CompilerParams(
                    collective_id=0, has_side_effects=True, vmem_limit_bytes=60 * 2**20
                ),
            )(b_factors, right_side, denom)
        )

    in_specs = (P("occ", "vir", "aux"), P("occ", "vir"), P("occ"), P("vir"))
    out_specs = (P("occ", "vir"), P("occ", "vir"))
    return jax.shard_map(shards, mesh=mesh, in_specs=in_specs, out_specs=out_specs, check_vma=False)
```

time: 363 us -> 125 us (0.34)
  blocking collectives: 151 us -> 0 us
  Pallas kernels: 0 us -> 120 us
  waiting for transfers between devices: 89.6 us -> 0 us
  matrix products: 52.4 us -> 0 us
  starting transfers between devices: 41.8 us -> 0 us
  between operations: 10.6 us -> 0.64 us
  local copies, waits for them, and re-layouts: 9.39 us -> 2.69 us
    pallas_call x0 -> x1, Pallas kernels: none -> 120 us  [shards(): pl.pallas_call(functools.partial(kernel, sizes), out_shape=[jax.ShapeDtyp...]
    all_to_all x6 -> x0, blocking collectives: 103 us -> none  [copy_for_each(): return lax.all_to_all(copies, axis, split_axis=0, concat_axis=0, tiled=True)]
    all_to_all x12 -> x0, waiting for transfers between devices: 89.6 us -> none  [the longest x6 72.9 us: copy_for_each(): return lax.all_to_all(copies, axis, split_axis=0, concat_axis=0, tiled=True)]
    dot_general x12 -> x0, matrix products: 52.4 us -> none  [the longest x3 15.9 us: respond(): jnp.einsum('jaq,ijq->ia', b_factors, moved, preferred_element_type=jnp.fl...]
    psum x6 -> x0, blocking collectives: 47.7 us -> none  [by_axis(): return functools.reduce(lax.psum, axes, array)]
    all_to_all x12 -> x0, starting transfers between devices: 41.8 us -> none  [the longest x6 21.7 us: copy_for_each(): return lax.all_to_all(copies, axis, split_axis=0, concat_axis=0, tiled=True)]
    broadcast_in_dim x12 -> x0, local copies, waits for them, and re-layouts: 6.84 us -> none  [copy_for_each(): copies = jnp.broadcast_to(array, (lax.axis_size(axis), *array.shape))]
  transfers between devices with their start and end apart: 12 -> 0, of which waited for: 12 -> 0; matrix products, arithmetic and copies ran while one was open for 8% -> 0% of each run, Pallas kernels for 0% -> 0%
where the time goes in v1:
time: 125 us
  Pallas kernels  120 us (96%)
  local copies, waits for them, and re-layouts  2.69 us (2%)
  other arithmetic  1.38 us (1%)
    pallas_call x1, Pallas kernels, shards(): pl.pallas_call(functools.partial(kernel, sizes), out_shape=[jax.ShapeDtyp...  120 us
    unnamed x2, local copies, waits for them, and re-layouts  2.69 us

profile of v1, /device:TPU:1, one launch (start us, length us, event | category | flops | bytes accessed | tf_op | source)
XLA Modules:
  0.0 124.8 jit_solution(6242028015994875541)
XLA Ops:
  0.6 1.4 %broadcast_subtract_fusion.denom_ref = f32[8,768]{1,0:T(8,128)} fusion(f32[8]{0:T(128)} %param.6, f32[768]{0:T(1024)} %param.7), kind=kLoop, calls=%fused_computation | loop fusion | flops 6144 | bytes 27680 | tf_op jit(solution)/shard_map/sub | solution.py:311
  2.0 120.0 %shard_map.59 = (f32[8,768]{1,0:T(8,128)}, f32[8,768]{1,0:T(8,128)}) custom-call(bf16[8,768,512]{2,1,0:T(8,128)(2,1)} %b_hbm.1, f32[8,768]{1,0:T(8,128)} %right_ref.1, f32[8,768]{1,0:T(8,128)} %broadcast_subtract_fusion.denom_ref), custom_call_target="tpu_custom_call" | custom-call | tf_op jit(solution)/shard_map/pallas_call | solution.py:316
  122.1 1.3 %copy.8 = f32[8,768]{1,0:T(8,128)} copy(f32[8,768]{1,0:T(8,128)} %get-tuple-element.4) | data formatting | bytes 49152
  123.4 1.3 %copy.9 = f32[8,768]{1,0:T(8,128)} copy(f32[8,768]{1,0:T(8,128)} %get-tuple-element.5) | data formatting | bytes 49152

commit v2 on v0

v2 whole, which is shorter than its diff:
```python
import functools

import jax
import jax.numpy as jnp
from jax import lax
from jax.experimental import pallas as pl
from jax.experimental.pallas import tpu as pltpu
from jax.sharding import PartitionSpec as P

ITERS = 3
MESH = pl.DeviceIdType.MESH
LANES = 128
ROWS = 8


def wait_bytes(ref, sem):
    pltpu.make_async_copy(ref, ref, sem).wait()


def kernel(
    sizes,
    b_hbm,
    right_hbm,
    occ_smem,
    vir_hbm,
    both_out,
    b_ref,
    right_ref,
    vir_ref,
    rd_ref,
    xh_ref,
    z_ref,
    x_ref,
    dir_ref,
    along_ref,
    p1_send,
    p1_recv,
    sums_ref,
    pairs_ref,
    diag_ref,
    gamma_ref,
    acc_ref,
    a_send,
    a_recv,
    b_recv,
    total_ref,
    da_recv,
    db_recv,
    dc_recv,
    b_sem,
    in_sem,
    sems,
):
    n_aux, n_occ, n_vir = sizes
    aux, occ, vir = lax.axis_index("aux"), lax.axis_index("occ"), lax.axis_index("vir")
    n_i, n_a, n_p = b_ref.shape
    tiles = n_a // LANES
    n_all = n_occ * n_i
    n_z, group = n_aux // 2, n_occ * 2
    per = tiles // 2
    z, core = aux // 2, lax.rem(aux, 2)
    plane = n_occ * n_vir
    quarter = n_p // n_vir
    here = occ * n_vir + vir
    spot = occ * 2 + core

    def device(aux_at, occ_at, vir_at):
        return {"aux": aux_at, "occ": occ_at, "vir": vir_at}

    def send(src, dst, send_sem, recv_sem, where):
        pltpu.make_async_remote_copy(
            src_ref=src,
            dst_ref=dst,
            send_sem=send_sem,
            recv_sem=recv_sem,
            device_id=where,
            device_id_type=MESH,
        ).start()

    def shifted(at, step, size):
        return lax.rem(at + step, size) if step else at

    def plane_peer(step):
        occ_at, vir_at = shifted(occ, step // n_vir, n_occ), shifted(vir, step % n_vir, n_vir)
        return occ_at * n_vir + vir_at, device(aux, occ_at, vir_at)

    def group_peer(step):
        occ_at, core_at = shifted(occ, step // 2, n_occ), shifted(core, step % 2, 2)
        return occ_at * 2 + core_at, device(z * 2 + core_at, occ_at, vir)

    def z_peer(step):
        return device(shifted(z, step, n_z) * 2 + core, occ, vir)

    def vir_peer(step):
        return device(aux, occ, shifted(vir, step, n_vir))

    def load(i):
        return pltpu.make_async_copy(b_hbm.at[i], b_ref.at[i], b_sem.at[i])

    inputs = [
        pltpu.make_async_copy(right_hbm, right_ref, in_sem.at[0]),
        pltpu.make_async_copy(vir_hbm, vir_ref, in_sem.at[1]),
    ]
    for copy in inputs:
        copy.start()
    for i in range(n_i):
        load(i).start()

    barrier = pltpu.get_barrier_semaphore()
    peers = [plane_peer(step)[1] for step in range(1, plane)]
    peers += [group_peer(step)[1] for step in range(1, group) if step % 2]
    peers += [z_peer(step) for step in range(1, n_z)]
    for peer in peers:
        pl.semaphore_signal(barrier, inc=1, device_id=peer, device_id_type=MESH)

    for copy in inputs:
        copy.wait()
    row = lax.broadcasted_iota(jnp.int32, (ROWS, LANES), 0)
    occ_tile = jnp.zeros((ROWS, LANES), jnp.float32)
    for i in range(ROWS):
        occ_tile = jnp.where(row == i, occ_smem[i], occ_tile)
    for k in range(tiles):
        cut = slice(k * LANES, (k + 1) * LANES)
        rd_ref[occ, 0, k] = right_ref[:, cut]
        rd_ref[occ, 1, k] = vir_ref[:, cut] - occ_tile

    pl.semaphore_wait(barrier, len(peers))

    for step in range(1, n_occ):
        at = rd_ref.at[occ]
        send(at, at, in_sem.at[2], in_sem.at[3], device(aux, shifted(occ, step, n_occ), vir))
    wait_bytes(rd_ref.at[pl.ds(0, n_occ - 1)], in_sem.at[3])

    z_ref[...] = jnp.zeros_like(z_ref)
    rz_now = alpha = None
    order = [0, 1] + [n_vir - 1 - step for step in range(n_vir - 2)]

    for turn in range(ITERS):
        sem = functools.partial(lambda turn, index: sems.at[turn, index], turn)

        x = rd_ref[:, 0] / rd_ref[:, 1]
        x_ref[...] = x
        for o in range(0, n_occ, 2):
            for k in range(tiles):
                both = jnp.concatenate([x[o, k], x[o + 1, k]], axis=0)
                xh_ref[o * ROWS : (o + 2) * ROWS, k * LANES : (k + 1) * LANES] = both.astype(jnp.bfloat16)

        xh = xh_ref[...]
        diag = jnp.zeros((ROWS, n_p), jnp.float32)
        wide = lax.broadcasted_iota(jnp.int32, (ROWS, n_p), 0)
        for i in range(0, n_i, 2):
            if turn == 0:
                load(i).wait()
                load(i + 1).wait()
            one = jnp.dot(xh, b_ref[i], preferred_element_type=jnp.float32)
            two = jnp.dot(xh, b_ref[i + 1], preferred_element_type=jnp.float32)
            for o in range(n_occ):
                rows = slice(o * ROWS, (o + 1) * ROWS)
                mine = wide + (occ - o) * n_all
                diag = diag + jnp.where(mine == i, one[rows], 0.0) + jnp.where(mine == i + 1, two[rows], 0.0)
                for q in range(n_vir):
                    cut = (rows, slice(q * quarter, (q + 1) * quarter))
                    both = jnp.concatenate([one[cut], two[cut]], axis=0).astype(jnp.bfloat16)
                    p1_send[turn, o * n_vir + q, i * ROWS : (i + 2) * ROWS, :] = both

        for step in range(1, plane):
            at, where = plane_peer(step)
            send(p1_send.at[turn, at], p1_recv.at[turn, here], sem(0), sem(1), where)
        gamma_ref[turn, here] = jnp.sum(diag, axis=0, keepdims=True)
        for step in range(1, plane):
            at = gamma_ref.at[turn, here]
            send(at, at, sem(2), sem(3), plane_peer(step)[1])
        p1_recv[turn, here] = p1_send[turn, here]
        wait_bytes(p1_recv.at[turn, pl.ds(0, plane - 1)], sem(1))

        for o in range(n_occ):
            total = p1_recv[turn, o * n_vir].astype(jnp.float32)
            for v in range(1, n_vir):
                total = total + p1_recv[turn, o * n_vir + v].astype(jnp.float32)
            sums_ref[o * n_i * ROWS : (o + 1) * n_i * ROWS, :] = total
        for j in range(ROWS):
            column_j = sums_ref[pl.ds(j, n_all, stride=ROWS), :]
            pairs_ref[turn, vir, j * n_all : (j + 1) * n_all, :] = column_j.astype(jnp.bfloat16)
        for step in range(1, n_vir):
            at = pairs_ref.at[turn, vir]
            send(at, at, sem(4), sem(16 + step), vir_peer(step))

        wait_bytes(gamma_ref.at[turn, pl.ds(0, plane - 1)], sem(3))
        gamma = functools.reduce(jnp.add, [gamma_ref[turn, s] for s in range(plane)])
        diag_ref[...] = gamma
        acc_ref[...] = jnp.zeros_like(acc_ref)
        tall = lax.broadcasted_iota(jnp.int32, (2 * ROWS, 2 * quarter), 0)

        for first in range(0, n_vir, 2):
            quarters = []
            for step in order[first : first + 2]:
                q = lax.rem(vir + n_vir - step, n_vir) if step else vir
                if step:
                    wait_bytes(pairs_ref.at[turn, q], sem(16 + step))
                quarters.append((q, pl.ds(pl.multiple_of(q * quarter, quarter), quarter)))
            gamma = jnp.concatenate([diag_ref[:, lanes] for _, lanes in quarters], axis=1)
            gamma = jnp.broadcast_to(gamma, tall.shape)
            total = acc_ref[...]
            for j in range(ROWS):
                rows = slice(j * n_all, (j + 1) * n_all)
                left = jnp.concatenate([pairs_ref[turn, q, rows, :] for q, _ in quarters], axis=1)
                below = jnp.where(tall == j, gamma, 0.0).astype(jnp.bfloat16)
                left = jnp.concatenate([left, below], axis=0)
                right = jnp.concatenate([b_ref[j, :, lanes] for _, lanes in quarters], axis=1)
                total = total + lax.dot_general(
                    left, right, (((1,), (1,)), ((), ())), preferred_element_type=jnp.float32
                )
            acc_ref[...] = total

        delta = jnp.zeros((ROWS, LANES), jnp.float32)
        for o in range(n_occ):
            scale = jnp.where(occ == o, 4.0, 0.0)
            for k in range(tiles):
                lanes = slice(k * LANES, (k + 1) * LANES)
                tile = scale * acc_ref[n_all : n_all + ROWS, lanes] - acc_ref[o * ROWS : (o + 1) * ROWS, lanes]
                a_send[turn, o * 2 + k // per, k % per] = tile
                delta = delta + tile * x_ref[o, k]
        for step in range(1, group):
            at, where = group_peer(step)
            send(a_send.at[turn, at], a_recv.at[turn, spot], sem(5), sem(6), where)
        da_recv[turn, spot] = jnp.sum(delta, axis=0, keepdims=True)
        for step in range(1, group):
            at = da_recv.at[turn, spot]
            send(at, at, sem(7), sem(8), group_peer(step)[1])
        a_recv[turn, spot] = a_send[turn, spot]
        r, d = rd_ref[:, 0], rd_ref[:, 1]
        flat = (n_occ * tiles, ROWS, LANES)
        rz_part = jnp.sum(jnp.sum((r * x_ref[...]).reshape(flat), axis=0), axis=0, keepdims=True)
        own = jnp.sum(jnp.sum((d * x_ref[...] * x_ref[...]).reshape(flat), axis=0), axis=0, keepdims=True)
        wait_bytes(a_recv.at[turn, pl.ds(0, group - 1)], sem(6))
        b_recv[turn, z] = functools.reduce(jnp.add, [a_recv[turn, s] for s in range(group)])
        for step in range(1, n_z):
            at = b_recv.at[turn, z]
            send(at, at, sem(9), sem(10), z_peer(step))
        wait_bytes(da_recv.at[turn, pl.ds(0, group - 1)], sem(8))
        db_recv[turn, z] = functools.reduce(jnp.add, [da_recv[turn, s] for s in range(group)])
        for step in range(1, n_z):
            at = db_recv.at[turn, z]
            send(at, at, sem(11), sem(12), z_peer(step))

        wait_bytes(b_recv.at[turn, pl.ds(0, n_z - 1)], sem(10))
        total_ref[turn, spot] = functools.reduce(jnp.add, [b_recv[turn, s] for s in range(n_z)])
        for step in range(1, group):
            at = total_ref.at[turn, spot]
            send(at, at, sem(13), sem(14), group_peer(step)[1])
        wait_bytes(db_recv.at[turn, pl.ds(0, n_z - 1)], sem(12))
        delta = functools.reduce(jnp.add, [db_recv[turn, s] for s in range(n_z)]) + own
        dc_recv[turn, vir] = jnp.concatenate([rz_part, delta], axis=0)
        for step in range(1, n_vir):
            at = dc_recv.at[turn, vir]
            send(at, at, sem(15), sem(16), vir_peer(step))
        wait_bytes(dc_recv.at[turn, pl.ds(0, n_vir - 1)], sem(16))
        dots = functools.reduce(jnp.add, [dc_recv[turn, v] for v in range(n_vir)])
        rz_next = jnp.sum(dots[0:1], axis=1, keepdims=True)
        product = jnp.sum(dots[1:2], axis=1, keepdims=True)
        if turn == 0:
            alpha = rz_next / product
        else:
            ratio = rz_next / rz_now
            alpha = rz_next / (product - ratio * rz_next / alpha)
        rz_now = rz_next

        wait_bytes(total_ref.at[turn, pl.ds(0, group - 1)], sem(14))
        if turn + 1 < ITERS:
            x = x_ref[...]
            image = rd_ref[:, 1] * x + total_ref[turn].reshape(x.shape)
            if turn == 0:
                wait_bytes(rd_ref.at[pl.ds(0, n_occ - 1)], in_sem.at[2])
                direction, along = x, image
            else:
                direction = x + ratio[None, None] * dir_ref[...]
                along = image + ratio[None, None] * along_ref[...]
            dir_ref[...] = direction
            along_ref[...] = along
            z_ref[...] += alpha[None, None] * direction
            rd_ref[:, 0] = rd_ref[:, 0] - alpha[None, None] * along
        else:
            for k in range(tiles):
                cut = slice(k * LANES, (k + 1) * LANES)
                x = x_ref[occ, k]
                image = rd_ref[occ, 1, k] * x + total_ref[turn, occ * 2 + k // per, k % per]
                both_out[0, :, cut] = z_ref[occ, k] + alpha * (x + ratio * dir_ref[occ, k])
                both_out[1, :, cut] = rd_ref[occ, 0, k] - alpha * (image + ratio * along_ref[occ, k])

    for turn in range(ITERS):
        wait_bytes(p1_send.at[turn, pl.ds(0, plane - 1)], sems.at[turn, 0])
        wait_bytes(gamma_ref.at[turn, pl.ds(0, plane - 1)], sems.at[turn, 2])
        wait_bytes(pairs_ref.at[turn, pl.ds(0, n_vir - 1)], sems.at[turn, 4])
        wait_bytes(a_send.at[turn, pl.ds(0, group - 1)], sems.at[turn, 5])
        wait_bytes(da_recv.at[turn, pl.ds(0, group - 1)], sems.at[turn, 7])
        wait_bytes(b_recv.at[turn, pl.ds(0, n_z - 1)], sems.at[turn, 9])
        wait_bytes(db_recv.at[turn, pl.ds(0, n_z - 1)], sems.at[turn, 11])
        wait_bytes(total_ref.at[turn, pl.ds(0, group - 1)], sems.at[turn, 13])
        wait_bytes(dc_recv.at[turn, pl.ds(0, n_vir - 1)], sems.at[turn, 15])


def solution(mesh):
    sizes = tuple(mesh.shape[name] for name in ("aux", "occ", "vir"))
    n_aux, n_occ, n_vir = sizes

    def shards(b_factors, right_side, occ_energy, vir_energy):
        n_i, n_a, n_p = b_factors.shape
        tiles = n_a // LANES
        plane, group, n_z = n_occ * n_vir, n_occ * 2, n_aux // 2
        n_all = n_occ * n_i
        f32, bf16 = jnp.float32, jnp.bfloat16
        whole = pltpu.VMEM((n_occ, tiles, ROWS, LANES), f32)
        anywhere = pl.BlockSpec(memory_space=pl.ANY)
        both = pl.pallas_call(
            functools.partial(kernel, sizes),
            out_shape=jax.ShapeDtypeStruct((2, n_i, n_a), f32),
            in_specs=[anywhere, anywhere, pl.BlockSpec(memory_space=pltpu.SMEM), anywhere],
            out_specs=pl.BlockSpec(memory_space=pltpu.VMEM),
            scratch_shapes=[
                pltpu.VMEM((n_i, n_a, n_p), bf16),
                pltpu.VMEM((n_i, n_a), f32),
                pltpu.VMEM((1, n_a), f32),
                pltpu.VMEM((n_occ, 2, tiles, ROWS, LANES), f32),
                pltpu.VMEM((n_all, n_a), bf16),
                whole,
                whole,
                whole,
                whole,
                pltpu.VMEM((ITERS, plane, n_i * ROWS, LANES), bf16),
                pltpu.VMEM((ITERS, plane, n_i * ROWS, LANES), bf16),
                pltpu.VMEM((n_all * ROWS, LANES), f32),
                pltpu.VMEM((ITERS, n_vir, n_all * ROWS, LANES), bf16),
                pltpu.VMEM((1, n_p), f32),
                pltpu.VMEM((ITERS, plane, 1, n_p), f32),
                pltpu.VMEM((n_all + 2 * ROWS, n_a), f32),
                pltpu.VMEM((ITERS, group, tiles // 2, ROWS, LANES), f32),
                pltpu.VMEM((ITERS, group, tiles // 2, ROWS, LANES), f32),
                pltpu.VMEM((ITERS, n_z, tiles // 2, ROWS, LANES), f32),
                pltpu.VMEM((ITERS, group, tiles // 2, ROWS, LANES), f32),
                pltpu.VMEM((ITERS, group, 1, LANES), f32),
                pltpu.VMEM((ITERS, n_z, 1, LANES), f32),
                pltpu.VMEM((ITERS, n_vir, 2, LANES), f32),
                pltpu.SemaphoreType.DMA((n_i,)),
                pltpu.SemaphoreType.DMA((4,)),
                pltpu.SemaphoreType.DMA((ITERS, 16 + n_vir)),
            ],
            compiler_params=pltpu.CompilerParams(
                collective_id=0, has_side_effects=True, vmem_limit_bytes=60 * 2**20
            ),
        )(b_factors, right_side, occ_energy, vir_energy.reshape(1, n_a))
        return both[0], both[1]

    in_specs = (P("occ", "vir", "aux"), P("occ", "vir"), P("occ"), P("vir"))
    out_specs = (P("occ", "vir"), P("occ", "vir"))
    return jax.shard_map(shards, mesh=mesh, in_specs=in_specs, out_specs=out_specs, check_vma=False)
```

time: 363 us -> 102 us (0.28)
  blocking collectives: 151 us -> 0 us
  Pallas kernels: 0 us -> 98.8 us
  waiting for transfers between devices: 89.6 us -> 0 us
  matrix products: 52.4 us -> 0 us
  starting transfers between devices: 41.8 us -> 0 us
  between operations: 10.6 us -> 0.64 us
  local copies, waits for them, and re-layouts: 9.39 us -> 2.64 us
  other arithmetic: 4.9 us -> 0 us
    all_to_all x6 -> x0, blocking collectives: 103 us -> none  [copy_for_each(): return lax.all_to_all(copies, axis, split_axis=0, concat_axis=0, tiled=True)]
    pallas_call x0 -> x1, Pallas kernels: none -> 98.8 us  [shards(): pl.pallas_call(functools.partial(kernel, sizes), out_shape=jax.ShapeDtype...]
    all_to_all x12 -> x0, waiting for transfers between devices: 89.6 us -> none  [the longest x6 72.9 us: copy_for_each(): return lax.all_to_all(copies, axis, split_axis=0, concat_axis=0, tiled=True)]
    dot_general x12 -> x0, matrix products: 52.4 us -> none  [the longest x3 15.9 us: respond(): jnp.einsum('jaq,ijq->ia', b_factors, moved, preferred_element_type=jnp.fl...]
    psum x6 -> x0, blocking collectives: 47.7 us -> none  [by_axis(): return functools.reduce(lax.psum, axes, array)]
    all_to_all x12 -> x0, starting transfers between devices: 41.8 us -> none  [the longest x6 21.7 us: copy_for_each(): return lax.all_to_all(copies, axis, split_axis=0, concat_axis=0, tiled=True)]
    broadcast_in_dim x12 -> x0, local copies, waits for them, and re-layouts: 6.84 us -> none  [copy_for_each(): copies = jnp.broadcast_to(array, (lax.axis_size(axis), *array.shape))]
  transfers between devices with their start and end apart: 12 -> 0, of which waited for: 12 -> 0; matrix products, arithmetic and copies ran while one was open for 8% -> 0% of each run, Pallas kernels for 0% -> 0%
where the time goes in v2:
time: 102 us
  Pallas kernels  98.8 us (97%)
  local copies, waits for them, and re-layouts  2.64 us (3%)
    pallas_call x1, Pallas kernels, shards(): pl.pallas_call(functools.partial(kernel, sizes), out_shape=jax.ShapeDtype...  98.8 us

profile of v2, /device:TPU:1, one launch (start us, length us, event | category | flops | bytes accessed | tf_op | source)
XLA Modules:
  0.0 102.1 jit_solution(10639297436849586045)
XLA Ops:
  0.6 1.3 %reshape.7.vir_hbm = f32[1,768]{1,0:T(1,128)} reshape(f32[768]{0:T(1024)} %param.7) | data formatting | bytes 6144 | tf_op jit(solution)/shard_map/reshape | solution.py:350
  1.9 98.8 %shard_map.59 = f32[2,8,768]{2,1,0:T(8,128)} custom-call(bf16[8,768,512]{2,1,0:T(8,128)(2,1)} %b_hbm.1, f32[8,768]{1,0:T(8,128)} %right_hbm.1, f32[8]{0:T(128)} %occ_smem.1, f32[1,768]{1,0:T(1,128)} %reshape.7.vir_hbm), custom_call_target="tpu_custom_call" | custom-call | tf_op jit(solution)/shard_map/pallas_call | solution.py:314
  100.7 1.4 %slice_bitcast_fusion = (f32[8,768]{1,0:T(8,128)}, f32[8,768]{1,0:T(8,128)}) fusion(f32[2,8,768]{2,1,0:T(8,128)} %shard_map.59), kind=kLoop, calls=%fused_computation | loop fusion | bytes 98304 | tf_op jit(solution)/shard_map/squeeze | solution.py:351
